TPU v7x, 32 devices: a whole 2x2x4 slice. The times are simulated.
32 devices in a mesh: dp: 4 (over y, core), cells: 8 (over z, x).
Axes of the slice: x: 2, y: 2, z: 4, core: 2. Of those that a mesh axis runs over, the one named last changes fastest.
Arguments:
- sensitivity: float32 [8192, 12288], P('dp', 'cells'), may hold values from -0.0546875 to 0.0546875
- observed: float32 [8192, 256], P('dp'), may hold values from -6 to 6
- models: float32 [12288, 256], P('cells'), may hold values from -6 to 6
- neighbour_map: int32 [4, 768], replicated, may hold values from 0 to 767, as said below
- edge_mask: int32 [12288], P('cells'), may hold values 0 or 1
Outputs:
- updated: float32 [12288, 256], P('cells')
Inputs may be any that keep to these rules, and one draw needn't show every extreme that they name: `neighbour_map`: each row k maps every cell of a periodic 32 by 24 plane grid, numbered in a drawn order, to its neighbour in one of the four grid directions; every row is a permutation.
All inputs are finite; a program needn't handle non-finite values. No bound on the sum of `edge_mask` on one device may be relied on, other than what follows from the above.
Results may differ from a plain program's by a relative error of at most 0.0001.
Values sent between devices are 32-bit elements; how exact they have to be, the bound alone decides.
A program may use at most 128 MiB of HBM per device.

v0:
```python
import jax
import jax.numpy as jnp
from jax import lax
from jax.sharding import PartitionSpec as P

ITERS = 2


def with_halo(cells, sides, width):
    for axis, dim in sides:
        count = lax.axis_size(axis)
        ends = count - 1
        head = lax.slice_in_dim(cells, 0, width, axis=dim)
        tail = lax.slice_in_dim(cells, cells.shape[dim] - width, cells.shape[dim], axis=dim)
        cells = jnp.concatenate(
            [
                lax.ppermute(tail, axis, [(i, (i + 1) % count) for i in range(ends)]),
                cells,
                lax.ppermute(head, axis, [((i + 1) % count, i) for i in range(ends)]),
            ],
            axis=dim,
        )
    return cells


def reweight(misfit):
    return misfit / jnp.maximum(jnp.abs(misfit), 1.0)


def smooth_local(current, neighbour_map, edge_mask):
    plane_cells = neighbour_map.shape[1]
    count = current.shape[0] // plane_cells
    planes = current.reshape(count, plane_cells, current.shape[1])
    padded = with_halo(planes, (("cells", 0),), 1)
    total = jnp.zeros_like(planes)
    for other in (padded[:-2], padded[2:]):
        diff = other - planes
        total = total + diff / jnp.sqrt(1.0 + diff * diff)
    for k in range(4):
        other = jnp.take(planes, neighbour_map[k], axis=1)
        diff = other - planes
        total = total + diff / jnp.sqrt(1.0 + diff * diff)
    scale = 1.0 - 0.75 * edge_mask.astype(jnp.float32).reshape(count, plane_cells, 1)
    return (total * scale).reshape(current.shape)


def local(sensitivity, observed, models, neighbour_map, edge_mask):
    current = models
    for step in range(ITERS):
        predicted = lax.psum(
            jnp.dot(
                sensitivity,
                current,
                precision=lax.Precision.HIGHEST,
                preferred_element_type=jnp.float32,
            ),
            "cells",
        )
        weighted = reweight(predicted - observed)
        smooth = smooth_local(current, neighbour_map, edge_mask)
        partial_grad = lax.dot_general(
            sensitivity,
            weighted,
            (((0,), (0,)), ((), ())),
            precision=lax.Precision.HIGHEST,
            preferred_element_type=jnp.float32,
        )
        gradient = lax.psum(partial_grad, "dp")
        current = current - 1.0 * gradient + 0.05 * smooth
    return current


def solution(mesh):
    return jax.shard_map(
        local,
        mesh=mesh,
        in_specs=(P("dp", "cells"), P("dp", None), P("cells", None), P(), P("cells")),
        out_specs=P("cells", None),
        check_vma=False,
    )
```

profile of v0, /device:TPU:0, one launch (start us, length us, event | category | flops | bytes accessed | tf_op | source)
XLA Modules:
  0.0 418.7 jit_solution(4675436302633939359)
XLA Ops:
  6.5 13.9 %fusion.16 = f32[2048,256]{1,0:T(8,128)} fusion(f32[2048,1536]{1,0:T(8,128)} %param.7, f32[1536,256]{1,0:T(8,128)} %param.9), kind=kOutput, calls=%fused_computation.72 | convolution fusion | flops 9663676416 | bytes 16252928 | tf_op jit(solution)/shard_map/dot_general | solution.py:51
  20.6 1.3 copy-done
  21.9 1.3 slice_bitcast_fusion.3
  23.1 5.7 %collective-permute-start = (f32[1,768,256]{2,1,0:T(8,128)}, f32[1,768,256]{2,1,0:T(8,128)}, u32[]{:S(2)}, u32[]{:S(2)}) collective-permute-start(f32[1,768,256]{2,1,0:T(8,128)} %get-tuple-element.12), channel_id=1, source_target_pairs={{0,1},{1,2},{2,3},{3,4},{4,5},{5,6},{6,7},{8,9},{9,10},{10,11},{11... | collective-permute-start | bytes 2359304 | tf_op jit(solution)/shard_map/ppermute | solution.py:17
  28.9 1.3 collective-permute-start.1
  30.2 1.2 copy.73
  31.5 4.0 gather_fusion.3
  35.5 4.0 gather_fusion.2
  39.6 4.0 gather_fusion.1
  43.6 4.1 gather_fusion
  47.7 96.1 %all-reduce.5.cloned.1.call-done = f32[2048,256]{1,0:T(8,128)} async-done(((f32[2048,256]{1,0:T(8,128)}), f32[2048,256]{1,0:T(8,128)}) %all-reduce.5.cloned.1.call-update) | async-done | bytes 2097168 | tf_op jit(solution)/shard_map/psum | solution.py:50
  143.8 25.0 %convolution_bitcast_fusion.2 = f32[1536,256]{1,0:T(8,128)} fusion(f32[2048,1536]{1,0:T(8,128)} %param.7, f32[2048,256]{1,0:T(8,128)} %all-reduce.5.cloned.1.call-done, f32[2048,256]{1,0:T(8,128)} %param.8), kind=kOutput, calls=%fused_computation.10 | convolution fusion | flops 9665773568 | bytes 18350080 | tf_op jit(solution)/shard_map/dot_general | solution.py:61
  168.8 0.0 all-reduce.9.cloned.1.call-start
  168.9 1.3 copy-done.1
  170.2 6.2 %multiply_multiply_fusion.1 = f32[2,768,256]{2,1,0:T(8,128)} fusion(f32[2,768,256]{2,1,0:T(8,128)S(1)} %bitcast.61, f32[768,2,256]{2,1,0:T(2,128)S(1)} %copy-done.1, f32[768,2,256]{2,1,0:T(2,128)} %gather_fusion.2, f32[768,2,256]{2,1,0:T(2,128)} %gather_fusion.1, f32[768,2,256]{2,1,0:T(2,128)} %gather_fusion, f32[1,768,256]{2,1,0:T(8,128)} %collective-permute-done.1, ...), kind=kLoop, calls=%fused_computation.46 | loop fusion | flops 14548992 | bytes 11019264 | tf_op jit(solution)/shard_map/mul | solution.py:69
  176.4 34.7 %all-reduce.7.cloned.1.call-done = f32[1536,256]{1,0:T(8,128)} async-done(((f32[1536,256]{1,0:T(8,128)}), f32[1536,256]{1,0:T(8,128)}) %all-reduce.7.cloned.1.call-update) | async-done | bytes 1572880 | tf_op jit(solution)/shard_map/psum | solution.py:68
  211.1 2.2 bitcast_add_fusion.1
  213.3 13.5 %convolution_bitcast_fusion.1 = f32[2048,256]{1,0:T(8,128)} fusion(f32[1536,256]{1,0:T(8,128)S(1)} %bitcast_add_fusion.1, f32[2048,1536]{1,0:T(8,128)} %param.7), kind=kOutput, calls=%fused_computation.9 | convolution fusion | flops 9663676416 | bytes 16252928 | tf_op jit(solution)/shard_map/dot_general | solution.py:51
  226.9 1.2 copy.83
  228.1 4.0 gather_fusion.7
  232.1 4.0 gather_fusion.6
  236.1 4.0 gather_fusion.5
  240.2 4.1 gather_fusion.4
  244.2 1.3 slice_bitcast_fusion.1
  245.5 4.2 %collective-permute-start.2 = (f32[1,768,256]{2,1,0:T(8,128)}, f32[1,768,256]{2,1,0:T(8,128)}, u32[]{:S(2)}, u32[]{:S(2)}) collective-permute-start(f32[1,768,256]{2,1,0:T(8,128)} %get-tuple-element.10), channel_id=1, source_target_pairs={{0,1},{1,2},{2,3},{3,4},{4,5},{5,6},{6,7},{8,9},{9,10},{10,11},{11... | collective-permute-start | bytes 2359304 | tf_op jit(solution)/shard_map/ppermute | solution.py:17
  249.7 1.3 collective-permute-start.3
  251.0 90.5 %all-reduce.9.cloned.1.call-done = f32[2048,256]{1,0:T(8,128)} async-done(((f32[2048,256]{1,0:T(8,128)}), f32[2048,256]{1,0:T(8,128)}) %all-reduce.9.cloned.1.call-update) | async-done | bytes 2097168 | tf_op jit(solution)/shard_map/psum | solution.py:50
  341.5 24.8 %convolution_bitcast_fusion = f32[1536,256]{1,0:T(8,128)} fusion(f32[2048,1536]{1,0:T(8,128)} %param.7, f32[2048,256]{1,0:T(8,128)} %all-reduce.9.cloned.1.call-done, f32[2048,256]{1,0:T(8,128)} %param.8), kind=kOutput, calls=%fused_computation.8 | convolution fusion | flops 9665773568 | bytes 18350080 | tf_op jit(solution)/shard_map/dot_general | solution.py:61
  366.3 1.4 copy-done.2
  367.7 6.1 %multiply_multiply_fusion = f32[2,768,256]{2,1,0:T(8,128)} fusion(f32[2,768,256]{2,1,0:T(8,128)S(1)} %bitcast.59, f32[768,2,256]{2,1,0:T(2,128)S(1)} %copy-done.2, f32[768,2,256]{2,1,0:T(2,128)} %gather_fusion.6, f32[768,2,256]{2,1,0:T(2,128)} %gather_fusion.5, f32[768,2,256]{2,1,0:T(2,128)} %gather_fusion.4, f32[1,768,256]{2,1,0:T(8,128)} %collective-permute-done.3, ...), kind=kLoop, calls=%fused_computation.45 | loop fusion | flops 14548992 | bytes 11019264 | tf_op jit(solution)/shard_map/mul | solution.py:69
  373.8 34.8 %all-reduce.11.cloned.1.call-done = f32[1536,256]{1,0:T(8,128)} async-done(((f32[1536,256]{1,0:T(8,128)}), f32[1536,256]{1,0:T(8,128)}) %all-reduce.11.cloned.1.call-update) | async-done | bytes 1572880 | tf_op jit(solution)/shard_map/psum | solution.py:68
  408.6 3.3 bitcast_add_fusion
  (29 shorter events, 0.3 us)
Async XLA Ops:
  6.5 137.2 %all-reduce.5.cloned.1.call-start = ((), (), s32[]{:S(2)}) async-start(), calls=%async_computation | async-start | bytes 4194304 | tf_op jit(solution)/shard_map/psum | solution.py:50
  20.5 1.4 copy-start
  20.5 9.7 %copy-start.4 = (s32[1536]{0:T(1024)S(1)}, s32[1536]{0:T(1024)}, u32[]{:S(2)}) copy-start(s32[1536]{0:T(1024)} %param.11) | copy-start | bytes 18436
  20.5 190.6 %all-reduce.7.cloned.1.call-start = ((), (), s32[]{:S(2)}) async-start(), calls=%async_computation.1 | async-start | bytes 3145728 | tf_op jit(solution)/shard_map/psum | solution.py:68
  23.1 145.7 %collective-permute-start = (f32[1,768,256]{2,1,0:T(8,128)}, f32[1,768,256]{2,1,0:T(8,128)}, u32[]{:S(2)}, u32[]{:S(2)}) collective-permute-start(f32[1,768,256]{2,1,0:T(8,128)} %get-tuple-element.12), channel_id=1, source_target_pairs={{0,1},{1,2},{2,3},{3,4},{4,5},{5,6},{6,7},{8,9},{9,10},{10,11},{11... | collective-permute-start | bytes 2359304 | tf_op jit(solution)/shard_map/ppermute | solution.py:17
  28.9 140.0 %collective-permute-start.1 = (f32[1,768,256]{2,1,0:T(8,128)}, f32[1,768,256]{2,1,0:T(8,128)}, u32[]{:S(2)}, u32[]{:S(2)}) collective-permute-start(f32[1,768,256]{2,1,0:T(8,128)} %get-tuple-element.13), channel_id=1, source_target_pairs={{1,0},{2,1},{3,2},{4,3},{5,4},{6,5},{7,6},{9,8},{10,9},{11,10},{12... | collective-permute-start | bytes 2359304 | tf_op jit(solution)/shard_map/ppermute | solution.py:19
  30.2 1.2 copy-start.3
  168.8 1.4 copy-start.1
  168.8 172.7 %all-reduce.9.cloned.1.call-start = ((), (), s32[]{:S(2)}) async-start(), calls=%async_computation.2 | async-start | bytes 4194304 | tf_op jit(solution)/shard_map/psum | solution.py:50
  226.8 181.8 %all-reduce.11.cloned.1.call-start = ((), (), s32[]{:S(2)}) async-start(), calls=%async_computation.3 | async-start | bytes 3145728 | tf_op jit(solution)/shard_map/psum | solution.py:68
  245.5 120.8 %collective-permute-start.2 = (f32[1,768,256]{2,1,0:T(8,128)}, f32[1,768,256]{2,1,0:T(8,128)}, u32[]{:S(2)}, u32[]{:S(2)}) collective-permute-start(f32[1,768,256]{2,1,0:T(8,128)} %get-tuple-element.10), channel_id=1, source_target_pairs={{0,1},{1,2},{2,3},{3,4},{4,5},{5,6},{6,7},{8,9},{9,10},{10,11},{11... | collective-permute-start | bytes 2359304 | tf_op jit(solution)/shard_map/ppermute | solution.py:17
  249.7 116.6 %collective-permute-start.3 = (f32[1,768,256]{2,1,0:T(8,128)}, f32[1,768,256]{2,1,0:T(8,128)}, u32[]{:S(2)}, u32[]{:S(2)}) collective-permute-start(f32[1,768,256]{2,1,0:T(8,128)} %get-tuple-element.11), channel_id=1, source_target_pairs={{1,0},{2,1},{3,2},{4,3},{5,4},{6,5},{7,6},{9,8},{10,9},{11,10},{12... | collective-permute-start | bytes 2359304 | tf_op jit(solution)/shard_map/ppermute | solution.py:19
  366.3 1.4 copy-start.2
Sparse Core Ops, SparseCore 0:
  20.6 123.1 all-reduce.4
  168.9 42.1 all-reduce.6
  227.0 114.5 all-reduce.8
  366.4 42.1 all-reduce.10
where the time goes:
time: 426 us; the launch traced here: 419 us
  waiting for transfers between devices  256 us (60%)
  matrix products  77.2 us (18%)
  local copies, waits for them, and re-layouts  41.2 us (10%)
  other arithmetic  17.9 us (4%)
  between operations  13.5 us (3%)
  starting transfers between devices  12.7 us (3%)
    psum x2, waiting for transfers between devices, local(): lax.psum(jnp.dot(sensitivity, current, precision=lax.Precision.HIGHEST, p...  187 us
    psum x2, waiting for transfers between devices, local(): gradient = lax.psum(partial_grad, 'dp')  69.5 us
    dot_general x2, matrix products, local(): lax.dot_general(sensitivity, weighted, (((0,), (0,)), ((), ())), precisio...  49.8 us
    gather x8, local copies, waits for them, and re-layouts, smooth_local(): other = jnp.take(planes, neighbour_map[k], axis=1)  32.2 us
    dot_general x2, matrix products, local(): jnp.dot(sensitivity, current, precision=lax.Precision.HIGHEST, preferred_...  27.5 us
    mul x2, other arithmetic, local(): current = current - 1.0 * gradient + 0.05 * smooth  12.3 us
    ppermute x2, starting transfers between devices, with_halo(): lax.ppermute(tail, axis, [(i, (i + 1) % count) for i in range(ends)])  9.98 us
  transfers between devices with their start and end apart: 8, of which 4 were waited for; matrix products, arithmetic and copies ran while one was open for 24% of the time, Pallas kernels for 0%

commit v1 on v0

--- a/solution.py
+++ b/solution.py
@@ -65,7 +65,11 @@
             precision=lax.Precision.HIGHEST,
             preferred_element_type=jnp.float32,
         )
-        gradient = lax.psum(partial_grad, "dp")
+        gradient = partial_grad
+        for hop in (1, 2):
+            gradient = gradient + lax.ppermute(
+                gradient, "dp", [(dev, dev ^ hop) for dev in range(4)]
+            )
         current = current - 1.0 * gradient + 0.05 * smooth
     return current
 

time: 426 us -> 405 us (0.951)
  waiting for transfers between devices: 256 us -> 238 us
    psum x2 -> x0, waiting for transfers between devices: 69.5 us -> none  [local(): gradient = lax.psum(partial_grad, 'dp')]
    ppermute x2, waiting for transfers between devices: 0.01 us -> 21.9 us  [with_halo(): lax.ppermute(tail, axis, [(i, (i + 1) % count) for i in range(ends)])]
    psum x2, waiting for transfers between devices: 187 us -> 207 us  [local(): lax.psum(jnp.dot(sensitivity, current, precision=lax.Precision.HIGHEST, p...]
    ppermute x0 -> x4, waiting for transfers between devices: none -> 8.9 us  [local(): lax.ppermute(gradient, 'dp', [(dev, dev ^ hop) for dev in range(4)])]
    add x0 -> x2, other arithmetic: none -> 4.59 us  [local(): gradient + lax.ppermute(gradient, 'dp', [(dev, dev ^ hop) for dev in rang...]
  transfers between devices with their start and end apart: 8 -> 10, of which waited for: 4 -> 6; matrix products, arithmetic and copies ran while one was open for 24% -> 13% of each run, Pallas kernels for 0% -> 0%
where the time goes in v1:
time: 405 us; the launch traced here: 402 us
  waiting for transfers between devices  238 us (59%)
  matrix products  76.4 us (19%)
  local copies, waits for them, and re-layouts  37.2 us (9%)
  other arithmetic  21.1 us (5%)
  starting transfers between devices  15.2 us (4%)
  between operations  13.8 us (3%)
    psum x2, waiting for transfers between devices, local(): lax.psum(jnp.dot(sensitivity, current, precision=lax.Precision.HIGHEST, p...  207 us
    dot_general x2, matrix products, local(): lax.dot_general(sensitivity, weighted, (((0,), (0,)), ((), ())), precisio...  48.9 us
    gather x8, local copies, waits for them, and re-layouts, smooth_local(): other = jnp.take(planes, neighbour_map[k], axis=1)  32 us
    dot_general x2, matrix products, local(): jnp.dot(sensitivity, current, precision=lax.Precision.HIGHEST, preferred_...  27.5 us
    ppermute x2, waiting for transfers between devices, with_halo(): lax.ppermute(tail, axis, [(i, (i + 1) % count) for i in range(ends)])  21.9 us
    mul x2, other arithmetic, local(): current = current - 1.0 * gradient + 0.05 * smooth  10.6 us
    ppermute x4, waiting for transfers between devices, local(): lax.ppermute(gradient, 'dp', [(dev, dev ^ hop) for dev in range(4)])  8.9 us
    ppermute x2, starting transfers between devices, with_halo(): lax.ppermute(tail, axis, [(i, (i + 1) % count) for i in range(ends)])  8.56 us
  transfers between devices with their start and end apart: 10, of which 6 were waited for; matrix products, arithmetic and copies ran while one was open for 13% of the time, Pallas kernels for 0%

profile of v1, /device:TPU:0, one launch (start us, length us, event | category | flops | bytes accessed | tf_op | source)
XLA Modules:
  0.0 401.8 jit_solution(3334599808174801294)
XLA Ops:
  6.5 13.9 %fusion.16 = f32[2048,256]{1,0:T(8,128)} fusion(f32[2048,1536]{1,0:T(8,128)} %param.7, f32[1536,256]{1,0:T(8,128)} %param.9), kind=kOutput, calls=%fused_computation.72 | convolution fusion | flops 9663676416 | bytes 16252928 | tf_op jit(solution)/shard_map/dot_general | solution.py:51
  20.8 104.8 %all-reduce.3.cloned.1.call-done = f32[2048,256]{1,0:T(8,128)} async-done(((f32[2048,256]{1,0:T(8,128)}), f32[2048,256]{1,0:T(8,128)}) %all-reduce.3.cloned.1.call-update) | async-done | bytes 2097168 | tf_op jit(solution)/shard_map/psum | solution.py:50
  125.7 24.6 %convolution_bitcast_fusion.2 = f32[1536,256]{1,0:T(8,128)} fusion(f32[2048,1536]{1,0:T(8,128)} %param.7, f32[2048,256]{1,0:T(8,128)} %all-reduce.3.cloned.1.call-done, f32[2048,256]{1,0:T(8,128)} %param.8), kind=kOutput, calls=%fused_computation.10 | convolution fusion | flops 9665773568 | bytes 18350080 | tf_op jit(solution)/shard_map/dot_general | solution.py:61
  150.3 1.3 slice_bitcast_fusion.3
  151.6 4.3 %collective-permute-start.2 = (f32[1,768,256]{2,1,0:T(8,128)}, f32[1,768,256]{2,1,0:T(8,128)}, u32[]{:S(2)}, u32[]{:S(2)}) collective-permute-start(f32[1,768,256]{2,1,0:T(8,128)} %get-tuple-element.12), channel_id=1, source_target_pairs={{0,1},{1,2},{2,3},{3,4},{4,5},{5,6},{6,7},{8,9},{9,10},{10,11},{11... | collective-permute-start | bytes 2359304 | tf_op jit(solution)/shard_map/ppermute | solution.py:17
  155.9 1.8 collective-permute-start.3
  157.8 1.2 copy.73
  159.1 4.0 gather_fusion.3
  163.1 3.2 add.94
  166.3 1.5 collective-permute-start.1
  167.8 4.0 %gather_fusion.2 = f32[768,2,256]{2,1,0:T(2,128)} fusion(f32[2,768,256]{2,0,1:T(2,128)S(1)} %copy.73, s32[1024]{0:T(1024)S(1)} %pad_clamp_fusion.1), kind=kCustom, calls=%fused_computation.2.clone | custom fusion | bytes 3148800 | tf_op jit(solution)/shard_map/jit(_take)/gather | solution.py:40
  171.8 4.0 gather_fusion.1
  175.8 4.0 gather_fusion
  179.9 9.7 %collective-permute-done.2 = f32[1,768,256]{2,1,0:T(8,128)} collective-permute-done((f32[1,768,256]{2,1,0:T(8,128)}, f32[1,768,256]{2,1,0:T(8,128)}, u32[]{:S(2)}, u32[]{:S(2)}) %collective-permute-start.2) | collective-permute-done | bytes 786464 | tf_op jit(solution)/shard_map/ppermute | solution.py:17
  189.6 5.3 %multiply_multiply_fusion.1 = f32[2,768,256]{2,1,0:T(8,128)S(1)} fusion(f32[2,768,256]{2,1,0:T(8,128)S(1)} %bitcast.61, f32[768,2,256]{2,1,0:T(2,128)} %gather_fusion.3, f32[768,2,256]{2,1,0:T(2,128)} %gather_fusion.2, f32[768,2,256]{2,1,0:T(2,128)} %gather_fusion.1, f32[768,2,256]{2,1,0:T(2,128)} %gather_fusion, f32[1,768,256]{2,1,0:T(8,128)} %collective-permute-done.3, ...), kind=kLoop, calls=%fused_computation.46 | loop fusion | flops 14548992 | bytes 11019264 | tf_op jit(solution)/shard_map/mul | solution.py:73
  194.9 8.2 %collective-permute-done.1 = f32[1536,256]{1,0:T(8,128)} collective-permute-done((f32[1536,256]{1,0:T(8,128)}, f32[1536,256]{1,0:T(8,128)}, u32[]{:S(2)}, u32[]{:S(2)}) %collective-permute-start.1) | collective-permute-done | bytes 1572896 | tf_op jit(solution)/shard_map/ppermute | solution.py:70
  203.1 2.4 bitcast_add_fusion.1
  205.5 13.5 %convolution_bitcast_fusion.1 = f32[2048,256]{1,0:T(8,128)} fusion(f32[1536,256]{1,0:T(8,128)S(1)} %bitcast_add_fusion.1, f32[2048,1536]{1,0:T(8,128)} %param.7), kind=kOutput, calls=%fused_computation.9 | convolution fusion | flops 9663676416 | bytes 16252928 | tf_op jit(solution)/shard_map/dot_general | solution.py:51
  219.1 102.5 %all-reduce.5.cloned.1.call-done = f32[2048,256]{1,0:T(8,128)} async-done(((f32[2048,256]{1,0:T(8,128)}), f32[2048,256]{1,0:T(8,128)}) %all-reduce.5.cloned.1.call-update) | async-done | bytes 2097168 | tf_op jit(solution)/shard_map/psum | solution.py:50
  321.5 24.3 %convolution_bitcast_fusion = f32[1536,256]{1,0:T(8,128)S(1)} fusion(f32[2048,1536]{1,0:T(8,128)} %param.7, f32[2048,256]{1,0:T(8,128)} %all-reduce.5.cloned.1.call-done, f32[2048,256]{1,0:T(8,128)} %param.8), kind=kOutput, calls=%fused_computation.8 | convolution fusion | flops 9665773568 | bytes 18350080 | tf_op jit(solution)/shard_map/dot_general | solution.py:61
  346.0 1.3 slice_bitcast_fusion.1
  347.3 4.3 %collective-permute-start.6 = (f32[1,768,256]{2,1,0:T(8,128)}, f32[1,768,256]{2,1,0:T(8,128)}, u32[]{:S(2)}, u32[]{:S(2)}) collective-permute-start(f32[1,768,256]{2,1,0:T(8,128)} %get-tuple-element.10), channel_id=1, source_target_pairs={{0,1},{1,2},{2,3},{3,4},{4,5},{5,6},{6,7},{8,9},{9,10},{10,11},{11... | collective-permute-start | bytes 2359304 | tf_op jit(solution)/shard_map/ppermute | solution.py:17
  351.6 1.5 collective-permute-start.7
  353.1 1.4 add.108
  354.4 1.5 collective-permute-start.5
  357.1 4.0 gather_fusion.7
  361.1 4.0 gather_fusion.6
  365.1 4.0 gather_fusion.5
  369.2 4.0 gather_fusion.4
  373.1 12.1 %collective-permute-done.6 = f32[1,768,256]{2,1,0:T(8,128)} collective-permute-done((f32[1,768,256]{2,1,0:T(8,128)}, f32[1,768,256]{2,1,0:T(8,128)}, u32[]{:S(2)}, u32[]{:S(2)}) %collective-permute-start.6) | collective-permute-done | bytes 786464 | tf_op jit(solution)/shard_map/ppermute | solution.py:17
  385.3 5.3 %multiply_multiply_fusion = f32[2,768,256]{2,1,0:T(8,128)S(1)} fusion(f32[2,768,256]{2,1,0:T(8,128)S(1)} %bitcast.59, f32[768,2,256]{2,1,0:T(2,128)} %gather_fusion.7, f32[768,2,256]{2,1,0:T(2,128)} %gather_fusion.6, f32[768,2,256]{2,1,0:T(2,128)} %gather_fusion.5, f32[768,2,256]{2,1,0:T(2,128)} %gather_fusion.4, f32[1,768,256]{2,1,0:T(8,128)} %collective-permute-done.7, ...), kind=kLoop, calls=%fused_computation.45 | loop fusion | flops 14548992 | bytes 11019264 | tf_op jit(solution)/shard_map/mul | solution.py:73
  391.3 3.5 bitcast_add_fusion
  (29 shorter events, 2.5 us)
Async XLA Ops:
  6.5 119.1 %all-reduce.3.cloned.1.call-start = ((), (), s32[]{:S(2)}) async-start(), calls=%async_computation | async-start | bytes 4194304 | tf_op jit(solution)/shard_map/psum | solution.py:50
  20.5 129.8 %copy-start = (f32[1536,256]{1,0:T(8,128)S(1)}, f32[1536,256]{1,0:T(8,128)}, u32[]{:S(2)}) copy-start(f32[1536,256]{1,0:T(8,128)} %param.9) | copy-start | bytes 4718596
  20.5 301.0 %all-reduce.5.cloned.1.call-start = ((), (), s32[]{:S(2)}) async-start(), calls=%async_computation.1 | async-start | bytes 4194304 | tf_op jit(solution)/shard_map/psum | solution.py:50
  150.3 7.5 %copy-start.1 = (s32[4,768]{1,0:T(4,128)S(1)}, s32[4,768]{1,0:T(4,128)}, u32[]{:S(2)}) copy-start(s32[4,768]{1,0:T(4,128)} %param.10) | copy-start | bytes 36868
  150.3 7.5 %copy-start.2 = (s32[1536]{0:T(1024)S(1)}, s32[1536]{0:T(1024)}, u32[]{:S(2)}) copy-start(s32[1536]{0:T(1024)} %param.11) | copy-start | bytes 18436
  150.3 12.8 %collective-permute-start = (f32[1536,256]{1,0:T(8,128)}, f32[1536,256]{1,0:T(8,128)}, u32[]{:S(2)}, u32[]{:S(2)}) collective-permute-start(f32[1536,256]{1,0:T(8,128)} %convolution_bitcast_fusion.2), channel_id=1, source_target_pairs={{0,8},{8,0},{16,24},{24,16},{1,9},{9,1},{17,25},{25,17},{2,10},{10... | collective-permute-start | bytes 4718600 | tf_op jit(solution)/shard_map/ppermute | solution.py:70
  151.6 38.0 %collective-permute-start.2 = (f32[1,768,256]{2,1,0:T(8,128)}, f32[1,768,256]{2,1,0:T(8,128)}, u32[]{:S(2)}, u32[]{:S(2)}) collective-permute-start(f32[1,768,256]{2,1,0:T(8,128)} %get-tuple-element.12), channel_id=1, source_target_pairs={{0,1},{1,2},{2,3},{3,4},{4,5},{5,6},{6,7},{8,9},{9,10},{10,11},{11... | collective-permute-start | bytes 2359304 | tf_op jit(solution)/shard_map/ppermute | solution.py:17
  155.9 33.7 %collective-permute-start.3 = (f32[1,768,256]{2,1,0:T(8,128)}, f32[1,768,256]{2,1,0:T(8,128)}, u32[]{:S(2)}, u32[]{:S(2)}) collective-permute-start(f32[1,768,256]{2,1,0:T(8,128)} %get-tuple-element.13), channel_id=1, source_target_pairs={{1,0},{2,1},{3,2},{4,3},{5,4},{6,5},{7,6},{9,8},{10,9},{11,10},{12... | collective-permute-start | bytes 2359304 | tf_op jit(solution)/shard_map/ppermute | solution.py:19
  166.3 36.8 %collective-permute-start.1 = (f32[1536,256]{1,0:T(8,128)}, f32[1536,256]{1,0:T(8,128)}, u32[]{:S(2)}, u32[]{:S(2)}) collective-permute-start(f32[1536,256]{1,0:T(8,128)} %add.94), channel_id=1, source_target_pairs={{0,16},{8,24},{16,0},{24,8},{1,17},{9,25},{17,1},{25,9},{2,18},{10... | collective-permute-start | bytes 4718600 | tf_op jit(solution)/shard_map/ppermute | solution.py:70
  345.9 7.2 %collective-permute-start.4 = (f32[1536,256]{1,0:T(8,128)S(1)}, f32[1536,256]{1,0:T(8,128)S(1)}, u32[]{:S(2)}, u32[]{:S(2)}) collective-permute-start(f32[1536,256]{1,0:T(8,128)S(1)} %convolution_bitcast_fusion), channel_id=1, source_target_pairs={{0,8},{8,0},{16,24},{24,16},{1,9},{9,1},{17,25},{25,17},{2,10},{10... | collective-permute-start | bytes 4718600 | tf_op jit(solution)/shard_map/ppermute | solution.py:70
  347.3 38.0 %collective-permute-start.6 = (f32[1,768,256]{2,1,0:T(8,128)}, f32[1,768,256]{2,1,0:T(8,128)}, u32[]{:S(2)}, u32[]{:S(2)}) collective-permute-start(f32[1,768,256]{2,1,0:T(8,128)} %get-tuple-element.10), channel_id=1, source_target_pairs={{0,1},{1,2},{2,3},{3,4},{4,5},{5,6},{6,7},{8,9},{9,10},{10,11},{11... | collective-permute-start | bytes 2359304 | tf_op jit(solution)/shard_map/ppermute | solution.py:17
  351.6 33.7 %collective-permute-start.7 = (f32[1,768,256]{2,1,0:T(8,128)}, f32[1,768,256]{2,1,0:T(8,128)}, u32[]{:S(2)}, u32[]{:S(2)}) collective-permute-start(f32[1,768,256]{2,1,0:T(8,128)} %get-tuple-element.11), channel_id=1, source_target_pairs={{1,0},{2,1},{3,2},{4,3},{5,4},{6,5},{7,6},{9,8},{10,9},{11,10},{12... | collective-permute-start | bytes 2359304 | tf_op jit(solution)/shard_map/ppermute | solution.py:19
  354.4 36.8 %collective-permute-start.5 = (f32[1536,256]{1,0:T(8,128)}, f32[1536,256]{1,0:T(8,128)}, u32[]{:S(2)}, u32[]{:S(2)}) collective-permute-start(f32[1536,256]{1,0:T(8,128)} %add.108), channel_id=1, source_target_pairs={{0,16},{8,24},{16,0},{24,8},{1,17},{9,25},{17,1},{25,9},{2,18},{10... | collective-permute-start | bytes 4718600 | tf_op jit(solution)/shard_map/ppermute | solution.py:70
Sparse Core Ops, SparseCore 0:
  20.6 105.0 all-reduce.2
  219.2 102.3 all-reduce.4
